TPU v7x, 32 devices: a whole 2x2x4 slice. The times are simulated.
32 devices in a mesh: dp: 8 (over z, y), tensor: 4 (over x, core).
Axes of the slice: x: 2, y: 2, z: 4, core: 2. Of those that a mesh axis runs over, the one named last changes fastest.
Arguments:
- tokens: bfloat16 [8192, 2048], P('dp'), may hold values from -6 to 6
- segment_ids: int32 [8, 1024], P('dp'), may hold values from 0 to 7, never falling along the last dimension, each value on 1 to 512 neighbouring positions
- attn_gain: bfloat16 [2048], P('dp'), may hold values from 0.25 to 1.75
- query_weight: bfloat16 [2048, 2048], P('dp', 'tensor'), may hold values from -0.125 to 0.125
- key_weight: bfloat16 [2048, 512], P('dp', 'tensor'), may hold values from -0.125 to 0.125
- value_weight: bfloat16 [2048, 512], P('dp', 'tensor'), may hold values from -0.125 to 0.125
- output_weight: bfloat16 [2048, 2048], P('tensor', 'dp'), may hold values from -0.5 to 0.5
- ffn_gain: bfloat16 [2048], P('dp'), may hold values from 0.25 to 1.75
- gate_weight: bfloat16 [2048, 8192], P('dp', 'tensor'), may hold values from -0.125 to 0.125
- up_weight: bfloat16 [2048, 8192], P('dp', 'tensor'), may hold values from -0.125 to 0.125
- down_weight: bfloat16 [8192, 2048], P('tensor', 'dp'), may hold values from -0.0625 to 0.0625
- cotangent: bfloat16 [8192, 2048], P('dp'), may hold values from -6 to 6
Outputs:
- layer_output: bfloat16 [8192, 2048], P('dp')
- tokens_grad: float32 [8192, 2048], P('dp')
- attn_gain_grad: float32 [2048], P('dp')
- query_weight_grad: float32 [2048, 2048], P('dp', 'tensor')
- key_weight_grad: float32 [2048, 512], P('dp', 'tensor')
- value_weight_grad: float32 [2048, 512], P('dp', 'tensor')
- output_weight_grad: float32 [2048, 2048], P('tensor', 'dp')
- ffn_gain_grad: float32 [2048], P('dp')
- gate_weight_grad: float32 [2048, 8192], P('dp', 'tensor')
- up_weight_grad: float32 [2048, 8192], P('dp', 'tensor')
- down_weight_grad: float32 [8192, 2048], P('tensor', 'dp')
Inputs may be any that keep to these rules, and one draw needn't show every extreme that they name: In each row of segment_ids the numbers never fall; each document spans 1 to 512 positions, and one spans exactly 512.
All inputs are finite; a program needn't handle non-finite values.
Results may differ from a plain program's by a relative error of at most 0.02.
Values may be sent and summed in bfloat16 or wider, within the bound.
A program may use at most 256 MiB of HBM per device.

v0:
```python
from functools import partial
import math
import jax
import jax.numpy as jnp
from jax import lax
from jax.sharding import PartitionSpec as P

HD = 64
epsilon = 1e-05


def rope_tables(segment_row, head_size):
    length = segment_row.shape[0]
    places = jnp.arange(length, dtype=jnp.int32)
    boundary = jnp.concatenate([jnp.ones((1,), dtype=bool), segment_row[1:] != segment_row[:-1]])
    starts = lax.cummax(jnp.where(boundary, places, 0), axis=0)
    position = (places - starts).astype(jnp.float32)
    half_size = head_size // 2
    exponent = jnp.arange(half_size, dtype=jnp.float32) * 2.0 / head_size
    inverse = 1.0 / 500000.0**exponent
    wavelen = 2.0 * math.pi / inverse
    smooth = (8192.0 / wavelen - 1.0) / 3.0
    scaled = jnp.where(
        wavelen < 2048.0,
        inverse,
        jnp.where(
            wavelen > 8192.0, inverse / 32.0, (1.0 - smooth) * inverse / 32.0 + smooth * inverse
        ),
    )
    angles = position[:, None] * scaled[None, :]
    cosine_table = jnp.cos(angles)
    sine_table = jnp.sin(angles)
    return (
        jnp.concatenate([cosine_table, cosine_table], axis=-1),
        jnp.concatenate([sine_table, sine_table], axis=-1),
    )


def rotate(values, cosine_table, sine_table):
    half_size = values.shape[-1] // 2
    turned = jnp.concatenate([-values[..., half_size:], values[..., :half_size]], axis=-1)
    return values * cosine_table + turned * sine_table


def rms_norm(values, gain_vector):
    factor = lax.rsqrt(jnp.mean(values * values, axis=-1, keepdims=True) + epsilon)
    return values * factor * gain_vector


def swiglu(gate_values, up_values):
    return jax.nn.silu(gate_values) * up_values


def contract_rows(left_side, right_side):
    return lax.dot_general(
        left_side, right_side, (((0,), (0,)), ((), ())), preferred_element_type=jnp.float32
    )


def contract_cols(left_side, right_side):
    return lax.dot_general(
        left_side, right_side, (((1,), (1,)), ((), ())), preferred_element_type=jnp.float32
    )


def block_scores(query_block, key_seq, segment_row, start_row):
    row_count = query_block.shape[0]
    length = key_seq.shape[0]
    score_scale = query_block.shape[-1] ** (-0.5)
    scores = (
        jnp.einsum("qkgd,skd->kgqs", query_block, key_seq, preferred_element_type=jnp.float32)
        * score_scale
    )
    row_ids = start_row + jnp.arange(row_count, dtype=jnp.int32)
    col_ids = jnp.arange(length, dtype=jnp.int32)
    same_doc = segment_row[start_row : start_row + row_count][:, None] == segment_row[None, :]
    allowed = same_doc & (col_ids[None, :] <= row_ids[:, None])
    return jnp.where(allowed, scores, -1000000000.0)


def attend_forward(operands):
    query_seq, key_seq, value_seq, segment_row = operands
    length, kv_local, head_size = key_seq.shape
    grouped = query_seq.reshape(length, kv_local, -1, head_size)
    block_rows = min(512, length)
    mixed_parts = []
    total_parts = []
    for start_row in range(0, length, block_rows):
        scores = block_scores(
            grouped[start_row : start_row + block_rows], key_seq, segment_row, start_row
        )
        row_max = jnp.max(scores, axis=-1, keepdims=True)
        log_total = jnp.log(jnp.sum(jnp.exp(scores - row_max), axis=-1, keepdims=True)) + row_max
        soft_low = jnp.exp(scores - log_total).astype(jnp.bfloat16)
        mixed_block = jnp.einsum(
            "kgqs,skd->qkgd", soft_low, value_seq, preferred_element_type=jnp.float32
        )
        mixed_parts.append(mixed_block.reshape(block_rows, -1).astype(jnp.bfloat16))
        total_parts.append(log_total)
    return (jnp.concatenate(mixed_parts, axis=0), jnp.concatenate(total_parts, axis=2))


def attend_backward(operands):
    query_seq, key_seq, value_seq, log_total, grad_seq, segment_row = operands
    length, kv_local, head_size = key_seq.shape
    grouped = query_seq.reshape(length, kv_local, -1, head_size)
    grad_grouped = grad_seq.reshape(length, kv_local, -1, head_size)
    block_rows = min(512, length)
    score_scale = head_size ** (-0.5)
    query_parts = []
    key_grad = jnp.zeros(key_seq.shape, jnp.float32)
    value_grad = jnp.zeros(value_seq.shape, jnp.float32)
    for start_row in range(0, length, block_rows):
        query_block = grouped[start_row : start_row + block_rows]
        grad_block = grad_grouped[start_row : start_row + block_rows]
        scores = block_scores(query_block, key_seq, segment_row, start_row)
        soft_weights = jnp.exp(scores - log_total[:, :, start_row : start_row + block_rows])
        soft_grad = jnp.einsum(
            "qkgd,skd->kgqs", grad_block, value_seq, preferred_element_type=jnp.float32
        )
        score_grad = (
            soft_weights * (soft_grad - jnp.sum(soft_weights * soft_grad, axis=-1, keepdims=True))
        ).astype(jnp.bfloat16)
        query_parts.append(
            jnp.einsum("kgqs,skd->qkgd", score_grad, key_seq, preferred_element_type=jnp.float32)
            * score_scale
        )
        key_grad = (
            key_grad
            + jnp.einsum(
                "kgqs,qkgd->skd", score_grad, query_block, preferred_element_type=jnp.float32
            )
            * score_scale
        )
        value_grad = value_grad + jnp.einsum(
            "kgqs,qkgd->skd",
            soft_weights.astype(jnp.bfloat16),
            grad_block,
            preferred_element_type=jnp.float32,
        )
    query_grad = jnp.concatenate(query_parts, axis=0).reshape(length, -1, head_size)
    return (query_grad, key_grad, value_grad)


def shards(
    tokens,
    segment_ids,
    attn_gain,
    query_weight,
    key_weight,
    value_weight,
    output_weight,
    ffn_gain,
    gate_weight,
    up_weight,
    down_weight,
    cotangent,
):
    gathered = (
        lax.all_gather(attn_gain, "dp", axis=0, tiled=True),
        lax.all_gather(query_weight, "dp", axis=0, tiled=True),
        lax.all_gather(key_weight, "dp", axis=0, tiled=True),
        lax.all_gather(value_weight, "dp", axis=0, tiled=True),
        lax.all_gather(output_weight, "dp", axis=1, tiled=True),
        lax.all_gather(ffn_gain, "dp", axis=0, tiled=True),
        lax.all_gather(gate_weight, "dp", axis=0, tiled=True),
        lax.all_gather(up_weight, "dp", axis=0, tiled=True),
        lax.all_gather(down_weight, "dp", axis=1, tiled=True),
    )
    seq_count, length = segment_ids.shape
    token_count = tokens.shape[0]
    tokens_float = tokens.astype(jnp.float32)
    cotangent_float = cotangent.astype(jnp.float32)
    attn_scale = gathered[0].astype(jnp.float32)
    ffn_scale = gathered[5].astype(jnp.float32)
    normed = rms_norm(tokens_float, attn_scale).astype(jnp.bfloat16)
    query_raw = jnp.dot(normed, gathered[1], preferred_element_type=jnp.float32)
    key_raw = jnp.dot(normed, gathered[2], preferred_element_type=jnp.float32)
    value_low = jnp.dot(normed, gathered[3], preferred_element_type=jnp.float32).astype(
        jnp.bfloat16
    )
    cosine_table, sine_table = jax.vmap(partial(rope_tables, head_size=HD))(segment_ids)
    cosine_wide = cosine_table[:, :, None, :]
    sine_wide = sine_table[:, :, None, :]
    query_shaped = query_raw.reshape(seq_count, length, -1, HD)
    key_shaped = key_raw.reshape(seq_count, length, -1, HD)
    query_low = rotate(query_shaped, cosine_wide, sine_wide).astype(jnp.bfloat16)
    key_low = rotate(key_shaped, cosine_wide, sine_wide).astype(jnp.bfloat16)
    value_seqs = value_low.reshape(seq_count, length, -1, HD)
    mixed_low, log_total = lax.map(attend_forward, (query_low, key_low, value_seqs, segment_ids))
    mixed_low = mixed_low.reshape(token_count, -1)
    attn_part = jnp.dot(mixed_low, gathered[4], preferred_element_type=jnp.float32)
    hidden_state = tokens_float + lax.psum(attn_part, "tensor")
    normed_two = rms_norm(hidden_state, ffn_scale).astype(jnp.bfloat16)
    gate_values = jnp.dot(normed_two, gathered[6], preferred_element_type=jnp.float32)
    up_values = jnp.dot(normed_two, gathered[7], preferred_element_type=jnp.float32)
    active = swiglu(gate_values, up_values).astype(jnp.bfloat16)
    ffn_part = jnp.dot(active, gathered[8], preferred_element_type=jnp.float32)
    layer_output = (
        hidden_state + lax.psum(ffn_part.astype(jnp.bfloat16), "tensor").astype(jnp.float32)
    ).astype(jnp.bfloat16)
    down_grad = contract_rows(active, cotangent)
    active_grad = contract_cols(cotangent, gathered[8])
    unused_value, swiglu_pull = jax.vjp(swiglu, gate_values, up_values)
    gate_grad, up_grad = swiglu_pull(active_grad)
    gate_low = gate_grad.astype(jnp.bfloat16)
    up_low = up_grad.astype(jnp.bfloat16)
    gate_weight_grad = contract_rows(normed_two, gate_low)
    up_weight_grad = contract_rows(normed_two, up_low)
    mlp_part = contract_cols(gate_low, gathered[6]) + contract_cols(up_low, gathered[7])
    normed_two_grad = lax.psum(mlp_part, "tensor")
    unused_second, second_pull = jax.vjp(rms_norm, hidden_state, ffn_scale)
    hidden_part, ffn_gain_grad = second_pull(normed_two_grad)
    hidden_grad = cotangent_float + hidden_part
    hidden_low = hidden_grad.astype(jnp.bfloat16)
    output_weight_grad = contract_rows(mixed_low, hidden_low)
    mixed_grad = contract_cols(hidden_low, gathered[4]).astype(jnp.bfloat16)
    query_grad, key_grad, value_grad = lax.map(
        attend_backward,
        (
            query_low,
            key_low,
            value_seqs,
            log_total,
            mixed_grad.reshape(seq_count, length, -1, HD),
            segment_ids,
        ),
    )
    unused_query, query_pull = jax.vjp(
        partial(rotate, cosine_table=cosine_wide, sine_table=sine_wide), query_shaped
    )
    unused_key, key_pull = jax.vjp(
        partial(rotate, cosine_table=cosine_wide, sine_table=sine_wide), key_shaped
    )
    query_raw_grad = query_pull(query_grad)[0].reshape(token_count, -1).astype(jnp.bfloat16)
    key_raw_grad = key_pull(key_grad)[0].reshape(token_count, -1).astype(jnp.bfloat16)
    value_raw_grad = value_grad.reshape(token_count, -1).astype(jnp.bfloat16)
    query_weight_grad = contract_rows(normed, query_raw_grad)
    key_weight_grad = contract_rows(normed, key_raw_grad)
    value_weight_grad = contract_rows(normed, value_raw_grad)
    attn_back_part = (
        contract_cols(query_raw_grad, gathered[1])
        + contract_cols(key_raw_grad, gathered[2])
        + contract_cols(value_raw_grad, gathered[3])
    )
    normed_grad = lax.psum(attn_back_part.astype(jnp.bfloat16), "tensor").astype(jnp.float32)
    unused_first, first_pull = jax.vjp(rms_norm, tokens_float, attn_scale)
    token_part, attn_gain_grad = first_pull(normed_grad)
    tokens_grad = hidden_grad + token_part
    summed = (
        lax.psum_scatter(
            attn_gain_grad.astype(jnp.bfloat16), "dp", scatter_dimension=0, tiled=True
        ).astype(jnp.float32),
        lax.psum_scatter(
            query_weight_grad.astype(jnp.bfloat16), "dp", scatter_dimension=0, tiled=True
        ).astype(jnp.float32),
        lax.psum_scatter(
            key_weight_grad.astype(jnp.bfloat16), "dp", scatter_dimension=0, tiled=True
        ).astype(jnp.float32),
        lax.psum_scatter(
            value_weight_grad.astype(jnp.bfloat16), "dp", scatter_dimension=0, tiled=True
        ).astype(jnp.float32),
        lax.psum_scatter(
            output_weight_grad.astype(jnp.bfloat16), "dp", scatter_dimension=1, tiled=True
        ).astype(jnp.float32),
        lax.psum_scatter(
            ffn_gain_grad.astype(jnp.bfloat16), "dp", scatter_dimension=0, tiled=True
        ).astype(jnp.float32),
        lax.psum_scatter(
            gate_weight_grad.astype(jnp.bfloat16), "dp", scatter_dimension=0, tiled=True
        ).astype(jnp.float32),
        lax.psum_scatter(
            up_weight_grad.astype(jnp.bfloat16), "dp", scatter_dimension=0, tiled=True
        ).astype(jnp.float32),
        lax.psum_scatter(
            down_grad.astype(jnp.bfloat16), "dp", scatter_dimension=1, tiled=True
        ).astype(jnp.float32),
    )
    attn_gain_total = summed[0]
    ffn_gain_total = summed[5]
    return (
        layer_output,
        tokens_grad,
        attn_gain_total,
        summed[1],
        summed[2],
        summed[3],
        summed[4],
        ffn_gain_total,
        summed[6],
        summed[7],
        summed[8],
    )


def solution(mesh):
    return jax.shard_map(
        shards,
        mesh=mesh,
        in_specs=(
            P("dp", None),
            P("dp", None),
            P("dp"),
            P("dp", "tensor"),
            P("dp", "tensor"),
            P("dp", "tensor"),
            P("tensor", "dp"),
            P("dp"),
            P("dp", "tensor"),
            P("dp", "tensor"),
            P("tensor", "dp"),
            P("dp", None),
        ),
        out_specs=(
            P("dp", None),
            P("dp", None),
            P("dp"),
            P("dp", "tensor"),
            P("dp", "tensor"),
            P("dp", "tensor"),
            P("tensor", "dp"),
            P("dp"),
            P("dp", "tensor"),
            P("dp", "tensor"),
            P("tensor", "dp"),
        ),
        check_vma=False,
    )
```

profile of v0, /device:TPU:0, one launch (start us, length us, event | category | flops | bytes accessed | tf_op | source)
XLA Modules:
  0.0 1853.7 jit_solution(15969643140244901022)
XLA Ops:
  15.5 22.5 %all-gather = bf16[8,1,256]{2,1,0:T(2,128)(2,1)S(1)} all-gather(bf16[1,1,256]{2,1,0:T(2,128)(2,1)S(1)} %reshape.443), channel_id=1, replica_groups=mesh['dp'=8,'tensor'=4] {'dp'}, dimensions={0}, use_global_device_ids=true | all-gather | bytes 4608 | tf_op jit(solution)/shard_map/all_gather | solution.py:160
  38.7 33.1 %all_gather.29 = bf16[2048,128]{1,0:T(8,128)(2,1)S(1)} all-gather(bf16[256,128]{1,0:T(8,128)(2,1)} %param.16), channel_id=1, replica_groups=mesh['dp'=8,'tensor'=4] {'dp'}, dimensions={0}, use_global_device_ids=true | all-gather | bytes 589824 | tf_op jit(solution)/shard_map/all_gather | solution.py:162
  71.8 32.3 %all_gather.28 = bf16[2048,128]{1,0:T(8,128)(2,1)S(1)} all-gather(bf16[256,128]{1,0:T(8,128)(2,1)} %param.17), channel_id=1, replica_groups=mesh['dp'=8,'tensor'=4] {'dp'}, dimensions={0}, use_global_device_ids=true | all-gather | bytes 589824 | tf_op jit(solution)/shard_map/all_gather | solution.py:163
  112.1 5.3 fusion.64
  118.3 7.7 fusion.11
  126.0 9.2 exponential_reduce_fusion
  135.3 7.3 fusion.10
  142.6 9.2 exponential_reduce_fusion.1
  151.8 8.4 convolution_convert_fusion.8
  166.7 7.5 fusion.41
  176.0 16.3 all-gather.1
  192.3 132.1 %all-reduce.12.cloned.1.call-done = f32[1024,2048]{1,0:T(8,128)} async-done(((f32[1024,2048]{1,0:T(8,128)}), f32[1024,2048]{1,0:T(8,128)}) %all-reduce.12.cloned.1.call-update) | async-done | bytes 8388624 | tf_op jit(solution)/shard_map/psum | solution.py:193
  324.5 5.7 multiply_reduce_fusion.2
  336.3 114.8 %all-gather.14.cloned.1.call-done = bf16[2048,2048]{1,0:T(8,128)(2,1)} async-done(((bf16[256,2048]{1,0:T(8,128)(2,1)}), bf16[2048,2048]{1,0:T(8,128)(2,1)}) %all-gather.14.cloned.1.call-update) | async-done | bytes 8388624 | tf_op jit(solution)/shard_map/all_gather | solution.py:167
  451.1 14.7 fusion.66
  465.8 110.0 %all-gather.12.cloned.1.call-done = bf16[2048,2048]{1,0:T(8,128)(2,1)} async-done(((bf16[256,2048]{1,0:T(8,128)(2,1)}), bf16[2048,2048]{1,0:T(8,128)(2,1)}) %all-gather.12.cloned.1.call-update) | async-done | bytes 8388624 | tf_op jit(solution)/shard_map/all_gather | solution.py:166
  575.8 14.6 fusion.65
  590.3 110.5 %all-gather.16.cloned.1.call-done = bf16[2048,2048]{1,0:T(8,128)(2,1)} async-done(((bf16[2048,256]{1,0:T(8,128)(2,1)}), bf16[2048,2048]{1,0:T(8,128)(2,1)}) %all-gather.16.cloned.1.call-update) | async-done | bytes 8388624 | tf_op jit(solution)/shard_map/all_gather | solution.py:168
  700.8 21.7 %multiply_convert_fusion = (bf16[1024,2048]{1,0:T(8,128)(2,1)}, bf16[1024,2048]{1,0:T(8,128)(2,1)}, bf16[1024,2048]{1,0:T(8,128)(2,1)}) fusion(f32[1024,2048]{1,0:T(8,128)} %fusion.65, f32[1024,2048]{1,0:T(8,128)} %fusion.66, bf16[1024,2048]{1,0:T(8,128)(2,1)} %param.23, bf16[2048,2048]{1,0:T(8,128)(2,1)} %all-gather.16.cloned.1.call-done), kind=kOutput, calls=%fused_computation.44 | convolution fusion | flops 8623489024 | bytes 41943040 | tf_op jit(solution)/shard_map/dot_general | solution.py:61
  722.5 13.1 fusion.67
  735.7 13.6 convolution_add_fusion
  751.1 149.5 %all-reduce.14.cloned.1.call-done = f32[1024,2048]{1,0:T(8,128)} async-done(((f32[1024,2048]{1,0:T(8,128)}), f32[1024,2048]{1,0:T(8,128)}) %all-reduce.14.cloned.1.call-update) | async-done | bytes 8388624 | tf_op jit(solution)/shard_map/psum | solution.py:211
  900.6 7.9 multiply_reduce_fusion
  908.5 9.6 fusion.17
  918.1 6.6 fusion.32
  925.4 5.2 convolution_bitcast_fusion
  930.6 9.4 fusion
  940.0 13.8 fusion.3
  953.8 8.6 fusion.40
  964.7 30.0 %fusion.2 = (bf16[2,4,512,1024]{2,3,1,0:T(8,128)(2,1)}, bf16[2,4,512,1024]{2,3,1,0:T(8,128)(2,1)}) fusion(f32[2,1024,512,4]{2,1,3,0:T(8,128)} %get-tuple-element.98, f32[2,1024,512,4]{2,1,3,0:T(8,128)} %get-tuple-element.94, f32[2,4,512]{2,1,0:T(4,128)S(1)} %copy-done.35, f32[2,4,512]{2,1,0:T(4,128)S(1)} %bitcast.237, ...), kind=kLoop, calls=%fused_computation.4 | loop fusion | flops 50331648 | bytes 85000192 | tf_op jit(solution)/shard_map/while/body/eval_jaxpr/convert_element_type | solution.py:123
  994.7 6.2 convolution_bitcast_fusion.2
  1006.0 7.1 convolution_convert_fusion.4
  1013.4 5.0 fusion.35
  1018.4 5.0 fusion.36
  1029.6 13.8 convolution_convert_fusion.3
  1051.0 14.1 convolution_convert_fusion
  1065.2 14.1 convolution_convert_fusion.1
  1079.6 14.2 convolution_convert_fusion.2
  1098.7 66.6 %reduce-scatter.14.cloned.1.call-done = bf16[512,256]{1,0:T(8,128)(2,1)} async-done(((bf16[512,2048]{1,0:T(8,128)(2,1)}), bf16[512,256]{1,0:T(8,128)(2,1)}) %reduce-scatter.14.cloned.1.call-update) | async-done | bytes 262160 | tf_op jit(solution)/shard_map/reduce_scatter | solution.py:263
  1167.0 69.8 %reduce-scatter.8.cloned.1.call-done = bf16[256,512]{1,0:T(8,128)(2,1)} async-done(((bf16[2048,512]{1,0:T(8,128)(2,1)}), bf16[256,512]{1,0:T(8,128)(2,1)}) %reduce-scatter.8.cloned.1.call-update) | async-done | bytes 262160 | tf_op jit(solution)/shard_map/reduce_scatter | solution.py:254
  1238.6 153.1 %all-reduce.16.cloned.1.call-done = (bf16[1024,2048]{1,0:T(8,128)(2,1)}, bf16[1024,2048]{1,0:T(8,128)(2,1)}) async-done(((bf16[1024,2048]{1,0:T(8,128)(2,1)}, bf16[1024,2048]{1,0:T(8,128)(2,1)}), (bf16[1024,2048]{1,0:T(8,128)(2,1)}, bf16[1024,2048]{1,0:T(8,128)(2,1)})) %all-reduce.16.cloned.1.call-update) | async-done | bytes 8388624 | tf_op jit(solution)/shard_map/psum | solution.py:200
  1391.7 5.9 fusion.13
  1397.7 22.9 %all-reduce.6 = (bf16[2048]{0:T(1024)(128)(2,1)S(1)}, bf16[2048]{0:T(1024)(128)(2,1)S(1)}) all-reduce(bf16[2048]{0:T(1024)(128)(2,1)S(1)} %get-tuple-element.54, bf16[2048]{0:T(1024)(128)(2,1)S(1)} %copy-done.41), channel_id=2, replica_groups=mesh['dp'=8,'tensor'=4] {'dp'}, use_global_device_ids=true, to_apply=%region_17.18.clone | all-reduce | flops 4096 | bytes 16384
  1421.9 8.6 add_convert_fusion.1
  1430.5 6.9 fusion.18
  1437.4 106.4 %reduce-scatter.20.cloned.1.call-done = bf16[2048,256]{1,0:T(8,128)(2,1)} async-done(((bf16[2048,2048]{1,0:T(8,128)(2,1)}), bf16[2048,256]{1,0:T(8,128)(2,1)}) %reduce-scatter.20.cloned.1.call-update) | async-done | bytes 1048592 | tf_op jit(solution)/shard_map/reduce_scatter | solution.py:275
  1546.5 147.4 %reduce-scatter.18.cloned.1.call-done = bf16[256,2048]{1,0:T(8,128)(2,1)} async-done(((bf16[2048,2048]{1,0:T(8,128)(2,1)}), bf16[256,2048]{1,0:T(8,128)(2,1)}) %reduce-scatter.18.cloned.1.call-update) | async-done | bytes 1048592 | tf_op jit(solution)/shard_map/reduce_scatter | solution.py:272
  1696.7 147.3 %reduce-scatter.16.cloned.1.call-done = bf16[256,2048]{1,0:T(8,128)(2,1)} async-done(((bf16[2048,2048]{1,0:T(8,128)(2,1)}), bf16[256,2048]{1,0:T(8,128)(2,1)}) %reduce-scatter.16.cloned.1.call-update) | async-done | bytes 1048592 | tf_op jit(solution)/shard_map/reduce_scatter | solution.py:269
  (210 shorter events, 73.1 us)
Async XLA Ops:
  7.2 104.9 %all-gather.8.cloned.1.call-start = ((), (), s32[]{:S(2)}) async-start(), calls=%async_computation.7 | async-start | bytes 2359296 | tf_op jit(solution)/shard_map/all_gather | solution.py:161
  7.9 158.7 %all-gather.10.cloned.1.call-start = ((), (), s32[]{:S(2)}) async-start(), calls=%async_computation.8 | async-start | bytes 2359296 | tf_op jit(solution)/shard_map/all_gather | solution.py:164
  8.7 315.8 %all-reduce.12.cloned.1.call-start = ((), (), s32[]{:S(2)}) async-start(), calls=%async_computation.9 | async-start | bytes 16777216 | tf_op jit(solution)/shard_map/psum | solution.py:193
  14.6 96.5 %copy-start.37 = (f32[1024]{0:T(1024)}, f32[1024]{0:T(1024)S(1)}, u32[]{:S(2)}) copy-start(f32[1024]{0:T(1024)S(1)} %fusion.50) | copy-start | bytes 12292
  38.0 73.1 %copy-start.33 = (f32[8,1,256]{2,1,0:T(1,128)}, f32[8,1,256]{2,1,0:T(1,128)S(1)}, u32[]{:S(2)}) copy-start(f32[8,1,256]{2,1,0:T(1,128)S(1)} %convert_element_type.247) | copy-start | bytes 24580
  38.6 65.6 %copy-start.26 = (f32[1,1024,32]{1,2,0:T(8,128)}, f32[1,1024,32]{1,2,0:T(8,128)S(1)}, u32[]{:S(2)}) copy-start(f32[1,1024,32]{1,2,0:T(8,128)S(1)} %get-tuple-element.87) | copy-start | bytes 393220
  38.6 65.6 %copy-start.28 = (f32[1,1024,32]{1,2,0:T(8,128)}, f32[1,1024,32]{1,2,0:T(8,128)S(1)}, u32[]{:S(2)}) copy-start(f32[1,1024,32]{1,2,0:T(8,128)S(1)} %get-tuple-element.88) | copy-start | bytes 393220
  38.6 79.0 %copy-start.24 = (f32[1024,64]{0,1:T(8,128)}, f32[1024,64]{0,1:T(8,128)S(1)}, u32[]{:S(2)}) copy-start(f32[1024,64]{0,1:T(8,128)S(1)} %maximum_bitcast_fusion) | copy-start | bytes 786436
  38.7 78.9 %copy-start.22 = (f32[1024,64]{0,1:T(8,128)}, f32[1024,64]{0,1:T(8,128)S(1)}, u32[]{:S(2)}) copy-start(f32[1024,64]{0,1:T(8,128)S(1)} %maximum_bitcast_fusion.1) | copy-start | bytes 786436
  71.8 39.3 %copy-start.15 = (bf16[2048,128]{1,0:T(8,128)(2,1)}, bf16[2048,128]{1,0:T(8,128)(2,1)S(1)}, u32[]{:S(2)}) copy-start(bf16[2048,128]{1,0:T(8,128)(2,1)S(1)} %all_gather.29) | copy-start | bytes 1572868
  111.9 48.3 %copy-start.8 = (pred[512,1024]{0,1:T(8,128)(4,1)}, pred[512,1024]{0,1:T(8,128)(4,1)S(1)}, u32[]{:S(2)}) copy-start(pred[512,1024]{0,1:T(8,128)(4,1)S(1)} %get-tuple-element.89) | copy-start | bytes 1572868
  112.0 23.2 %copy-start.11 = (bf16[1024,2,64,1]{0,2,3,1:T(8,128)(2,1)}, bf16[1024,2,64,1]{0,2,3,1:T(8,128)(2,1)S(1)}, u32[]{:S(2)}) copy-start(bf16[1024,2,64,1]{0,2,3,1:T(8,128)(2,1)S(1)} %fusion.46) | copy-start | bytes 786436
  118.3 7.8 copy-start.19
  118.3 17.0 copy-start.17
  151.8 8.4 copy-start.31
  151.8 10.7 copy-start
  166.6 7.6 copy-start.47
  174.2 276.9 %all-gather.14.cloned.1.call-start = ((), (), s32[]{:S(2)}) async-start(), calls=%async_computation.11 | async-start | bytes 9437184 | tf_op jit(solution)/shard_map/all_gather | solution.py:167
  174.8 401.0 %all-gather.12.cloned.1.call-start = ((), (), s32[]{:S(2)}) async-start(), calls=%async_computation.10 | async-start | bytes 9437184 | tf_op jit(solution)/shard_map/all_gather | solution.py:166
  175.4 525.4 %all-gather.16.cloned.1.call-start = ((), (), s32[]{:S(2)}) async-start(), calls=%async_computation.12 | async-start | bytes 9437184 | tf_op jit(solution)/shard_map/all_gather | solution.py:168
  176.0 724.6 %all-reduce.14.cloned.1.call-start = ((), (), s32[]{:S(2)}) async-start(), calls=%async_computation.13 | async-start | bytes 16777216 | tf_op jit(solution)/shard_map/psum | solution.py:211
  722.5 13.2 copy-start.51
  749.4 346.3 %reduce-scatter.12.cloned.1.call-start = ((), (), s32[]{:S(2)}) async-start(), calls=%async_computation.16 | async-start | bytes 589824 | tf_op jit(solution)/shard_map/reduce_scatter | solution.py:260
  900.6 7.9 copy-start.21
  908.5 9.6 copy-start.43
  908.5 16.3 slice-start
  908.5 16.3 slice-start.1
  908.5 16.3 slice-start.2
  930.6 9.4 copy-start.9
  940.0 13.8 copy-start.32
  940.0 13.8 copy-start.50
  953.8 8.7 copy-start.5
  953.8 10.9 copy-start.35
  964.6 132.6 %reduce-scatter.10.cloned.1.call-start = ((), (), s32[]{:S(2)}) async-start(), calls=%async_computation.15 | async-start | bytes 589824 | tf_op jit(solution)/shard_map/reduce_scatter | solution.py:257
  964.7 30.0 %copy-start.20 = (bf16[1,512,8,64]{1,3,2,0:T(8,128)(2,1)S(1)}, bf16[1,512,8,64]{1,3,2,0:T(8,128)(2,1)}, u32[]{:S(2)}) copy-start(bf16[1,512,8,64]{1,3,2,0:T(8,128)(2,1)} %copy-done.19) | copy-start | bytes 1572868
  1006.0 159.3 %reduce-scatter.14.cloned.1.call-start = ((), (), s32[]{:S(2)}) async-start(), calls=%async_computation.17 | async-start | bytes 2359296 | tf_op jit(solution)/shard_map/reduce_scatter | solution.py:263
  1013.1 223.7 %reduce-scatter.8.cloned.1.call-start = ((), (), s32[]{:S(2)}) async-start(), calls=%async_computation.14 | async-start | bytes 2359296 | tf_op jit(solution)/shard_map/reduce_scatter | solution.py:254
  1029.5 362.2 %all-reduce.16.cloned.1.call-start = ((), (), s32[]{:S(2)}) async-start(), calls=%async_computation.21 | async-start | bytes 16777216 | tf_op jit(solution)/shard_map/psum | solution.py:200
  1029.6 13.9 copy-start.16
  1050.7 493.1 %reduce-scatter.20.cloned.1.call-start = ((), (), s32[]{:S(2)}) async-start(), calls=%async_computation.20 | async-start | bytes 9437184 | tf_op jit(solution)/shard_map/reduce_scatter | solution.py:275
  1065.2 628.8 %reduce-scatter.18.cloned.1.call-start = ((), (), s32[]{:S(2)}) async-start(), calls=%async_computation.19 | async-start | bytes 9437184 | tf_op jit(solution)/shard_map/reduce_scatter | solution.py:272
  1079.3 764.7 %reduce-scatter.16.cloned.1.call-start = ((), (), s32[]{:S(2)}) async-start(), calls=%async_computation.18 | async-start | bytes 9437184 | tf_op jit(solution)/shard_map/reduce_scatter | solution.py:269
  1093.8 298.0 %copy-start.34 = (f32[8,1,256]{2,1,0:T(1,128)S(1)}, f32[8,1,256]{2,1,0:T(1,128)}, u32[]{:S(2)}) copy-start(f32[8,1,256]{2,1,0:T(1,128)} %copy-done.33) | copy-start | bytes 24580
  1093.8 298.0 %copy-start.38 = (f32[1024]{0:T(1024)S(1)}, f32[1024]{0:T(1024)}, u32[]{:S(2)}) copy-start(f32[1024]{0:T(1024)} %copy-done.37) | copy-start | bytes 12292
  1093.8 303.9 %copy-start.41 = (bf16[2048]{0:T(1024)(128)(2,1)S(1)}, bf16[2048]{0:T(1024)(128)(2,1)}, u32[]{:S(2)}) copy-start(bf16[2048]{0:T(1024)(128)(2,1)} %get-tuple-element.52) | copy-start | bytes 12292
  1093.8 328.1 %copy-start.40 = (f32[1024]{0:T(1024)S(1)}, f32[1024]{0:T(1024)}, u32[]{:S(2)}) copy-start(f32[1024]{0:T(1024)} %copy-done.39) | copy-start | bytes 12292
  1421.9 8.6 copy-start.2
  1421.9 8.6 copy-start.10
  (23 other events, 86.4 us)
Sparse Core Ops, SparseCore 0:
  10.1 57.9 all-gather.7
  70.1 52.7 all-gather.9
  174.3 150.0 all-reduce.11
  326.4 124.6 all-gather.13
  453.1 122.6 all-gather.11
  577.7 123.1 all-gather.15
  749.5 151.0 all-reduce.13
  964.7 62.7 reduce-scatter.11
  1031.5 61.6 reduce-scatter.9
  1097.1 68.1 reduce-scatter.13
  1169.4 67.4 reduce-scatter.7
  1239.8 151.8 all-reduce.15
  1395.4 148.4 reduce-scatter.19
  1547.3 146.5 reduce-scatter.17
  1697.4 146.5 reduce-scatter.15
where the time goes:
time: 1860 us; the launch traced here: 1850 us
  waiting for transfers between devices  1310 us (70%)
  matrix products  262 us (14%)
  blocking collectives  127 us (7%)
  other arithmetic  124 us (7%)
    psum x1, waiting for transfers between devices, shards(): lax.psum(ffn_part.astype(jnp.bfloat16), 'tensor').astype(jnp.float32)  153 us
    psum x1, waiting for transfers between devices, shards(): normed_two_grad = lax.psum(mlp_part, 'tensor')  150 us
    reduce_scatter x1, waiting for transfers between devices, shards(): lax.psum_scatter(up_weight_grad.astype(jnp.bfloat16), 'dp', scatter_dimen...  147 us
    reduce_scatter x1, waiting for transfers between devices, shards(): lax.psum_scatter(gate_weight_grad.astype(jnp.bfloat16), 'dp', scatter_dim...  147 us
    psum x1, waiting for transfers between devices, shards(): hidden_state = tokens_float + lax.psum(attn_part, 'tensor')  132 us
    all_gather x1, waiting for transfers between devices, shards(): lax.all_gather(up_weight, 'dp', axis=0, tiled=True)  115 us
    all_gather x1, waiting for transfers between devices, shards(): lax.all_gather(down_weight, 'dp', axis=1, tiled=True)  110 us
    all_gather x1, waiting for transfers between devices, shards(): lax.all_gather(gate_weight, 'dp', axis=0, tiled=True)  110 us
  transfers between devices with their start and end apart: 15, of which 11 were waited for; matrix products, arithmetic and copies ran while one was open for 14% of the time, Pallas kernels for 0%

commit v1 on v0

--- a/solution.py
+++ b/solution.py
@@ -208,7 +208,7 @@
     gate_weight_grad = contract_rows(normed_two, gate_low)
     up_weight_grad = contract_rows(normed_two, up_low)
     mlp_part = contract_cols(gate_low, gathered[6]) + contract_cols(up_low, gathered[7])
-    normed_two_grad = lax.psum(mlp_part, "tensor")
+    normed_two_grad = jnp.sum(lax.all_gather(mlp_part, "tensor"), axis=0)
     unused_second, second_pull = jax.vjp(rms_norm, hidden_state, ffn_scale)
     hidden_part, ffn_gain_grad = second_pull(normed_two_grad)
     hidden_grad = cotangent_float + hidden_part

time: 1860 us -> 1850 us (level)
  waiting for transfers between devices: 1310 us -> 1270 us
    all_gather x0 -> x1, waiting for transfers between devices: none -> 155 us  [shards(): normed_two_grad = jnp.sum(lax.all_gather(mlp_part, 'tensor'), axis=0)]
    psum x1 -> x0, waiting for transfers between devices: 150 us -> none  [shards(): normed_two_grad = lax.psum(mlp_part, 'tensor')]
    reduce_scatter x1, waiting for transfers between devices: 106 us -> 0.02 us  [shards(): lax.psum_scatter(down_grad.astype(jnp.bfloat16), 'dp', scatter_dimension=...]
    reduce_scatter x1, waiting for transfers between devices: 0.01 us -> 63.9 us  [shards(): lax.psum_scatter(key_weight_grad.astype(jnp.bfloat16), 'dp', scatter_dime...]
    reduce_scatter x1, waiting for transfers between devices: 0.02 us -> 62.9 us  [shards(): lax.psum_scatter(value_weight_grad.astype(jnp.bfloat16), 'dp', scatter_di...]
    reduce_scatter x1, waiting for transfers between devices: 69.8 us -> 27.5 us  [shards(): lax.psum_scatter(query_weight_grad.astype(jnp.bfloat16), 'dp', scatter_di...]
    reduce_scatter x1, waiting for transfers between devices: 147 us -> 125 us  [shards(): lax.psum_scatter(up_weight_grad.astype(jnp.bfloat16), 'dp', scatter_dimen...]
  transfers between devices with their start and end apart: 15 -> 15, of which waited for: 11 -> 12; matrix products, arithmetic and copies ran while one was open for 14% -> 19% of each run, Pallas kernels for 0% -> 0%
where the time goes in v1:
time: 1850 us; the launch traced here: 1840 us
  waiting for transfers between devices  1270 us (69%)
  matrix products  271 us (15%)
  other arithmetic  140 us (8%)
  blocking collectives  126 us (7%)
    all_gather x1, waiting for transfers between devices, shards(): normed_two_grad = jnp.sum(lax.all_gather(mlp_part, 'tensor'), axis=0)  155 us
    psum x1, waiting for transfers between devices, shards(): lax.psum(ffn_part.astype(jnp.bfloat16), 'tensor').astype(jnp.float32)  153 us
    reduce_scatter x1, waiting for transfers between devices, shards(): lax.psum_scatter(gate_weight_grad.astype(jnp.bfloat16), 'dp', scatter_dim...  147 us
    psum x1, waiting for transfers between devices, shards(): hidden_state = tokens_float + lax.psum(attn_part, 'tensor')  132 us
    reduce_scatter x1, waiting for transfers between devices, shards(): lax.psum_scatter(up_weight_grad.astype(jnp.bfloat16), 'dp', scatter_dimen...  125 us
    all_gather x1, waiting for transfers between devices, shards(): lax.all_gather(up_weight, 'dp', axis=0, tiled=True)  115 us
    all_gather x1, waiting for transfers between devices, shards(): lax.all_gather(down_weight, 'dp', axis=1, tiled=True)  111 us
    all_gather x1, waiting for transfers between devices, shards(): lax.all_gather(gate_weight, 'dp', axis=0, tiled=True)  110 us
  transfers between devices with their start and end apart: 15, of which 12 were waited for; matrix products, arithmetic and copies ran while one was open for 19% of the time, Pallas kernels for 0%

profile of v1, /device:TPU:0, one launch (start us, length us, event | category | flops | bytes accessed | tf_op | source)
XLA Modules:
  0.0 1838.6 jit_solution(9054107256641903166)
XLA Ops:
  15.5 22.5 %all-gather.1 = bf16[8,1,256]{2,1,0:T(2,128)(2,1)S(1)} all-gather(bf16[1,1,256]{2,1,0:T(2,128)(2,1)S(1)} %reshape.444), channel_id=1, replica_groups=mesh['dp'=8,'tensor'=4] {'dp'}, dimensions={0}, use_global_device_ids=true | all-gather | bytes 4608 | tf_op jit(solution)/shard_map/all_gather | solution.py:160
  38.7 33.1 %all_gather.35 = bf16[2048,128]{1,0:T(8,128)(2,1)S(1)} all-gather(bf16[256,128]{1,0:T(8,128)(2,1)} %param.16), channel_id=1, replica_groups=mesh['dp'=8,'tensor'=4] {'dp'}, dimensions={0}, use_global_device_ids=true | all-gather | bytes 589824 | tf_op jit(solution)/shard_map/all_gather | solution.py:162
  71.8 32.3 %all_gather.34 = bf16[2048,128]{1,0:T(8,128)(2,1)S(1)} all-gather(bf16[256,128]{1,0:T(8,128)(2,1)} %param.17), channel_id=1, replica_groups=mesh['dp'=8,'tensor'=4] {'dp'}, dimensions={0}, use_global_device_ids=true | all-gather | bytes 589824 | tf_op jit(solution)/shard_map/all_gather | solution.py:163
  118.5 7.7 fusion.11
  126.2 9.2 exponential_reduce_fusion
  135.4 7.2 fusion.10
  142.7 9.2 exponential_reduce_fusion.1
  151.9 8.3 convolution_convert_fusion.8
  166.7 7.5 fusion.41
  176.1 16.3 all-gather.2
  192.4 132.1 %all-reduce.11.cloned.1.call-done = f32[1024,2048]{1,0:T(8,128)} async-done(((f32[1024,2048]{1,0:T(8,128)}), f32[1024,2048]{1,0:T(8,128)}) %all-reduce.11.cloned.1.call-update) | async-done | bytes 8388624 | tf_op jit(solution)/shard_map/psum | solution.py:193
  324.5 5.7 multiply_reduce_fusion.2
  336.4 114.8 %all-gather.16.cloned.1.call-done = bf16[2048,2048]{1,0:T(8,128)(2,1)} async-done(((bf16[256,2048]{1,0:T(8,128)(2,1)}), bf16[2048,2048]{1,0:T(8,128)(2,1)}) %all-gather.16.cloned.1.call-update) | async-done | bytes 8388624 | tf_op jit(solution)/shard_map/all_gather | solution.py:167
  451.1 14.7 fusion.66
  465.9 109.9 %all-gather.14.cloned.1.call-done = bf16[2048,2048]{1,0:T(8,128)(2,1)} async-done(((bf16[256,2048]{1,0:T(8,128)(2,1)}), bf16[2048,2048]{1,0:T(8,128)(2,1)}) %all-gather.14.cloned.1.call-update) | async-done | bytes 8388624 | tf_op jit(solution)/shard_map/all_gather | solution.py:166
  575.8 14.5 fusion.65
  590.3 110.6 %all-gather.18.cloned.1.call-done = bf16[2048,2048]{1,0:T(8,128)(2,1)} async-done(((bf16[2048,256]{1,0:T(8,128)(2,1)}), bf16[2048,2048]{1,0:T(8,128)(2,1)}) %all-gather.18.cloned.1.call-update) | async-done | bytes 8388624 | tf_op jit(solution)/shard_map/all_gather | solution.py:168
  700.9 21.8 %multiply_convert_fusion = (bf16[1024,2048]{1,0:T(8,128)(2,1)}, bf16[1024,2048]{1,0:T(8,128)(2,1)}, bf16[1024,2048]{1,0:T(8,128)(2,1)}) fusion(f32[1024,2048]{1,0:T(8,128)} %fusion.65, f32[1024,2048]{1,0:T(8,128)} %fusion.66, bf16[1024,2048]{1,0:T(8,128)(2,1)} %param.23, bf16[2048,2048]{1,0:T(8,128)(2,1)} %all-gather.18.cloned.1.call-done), kind=kOutput, calls=%fused_computation.44 | convolution fusion | flops 8623489024 | bytes 41943040 | tf_op jit(solution)/shard_map/dot_general | solution.py:61
  722.7 13.1 fusion.67
  735.8 13.6 convolution_add_fusion
  749.5 14.2 convolution_convert_fusion
  763.8 15.5 convolution_convert_fusion.1
  779.4 14.1 convolution_convert_fusion.2
  794.5 154.8 %all-gather.20.cloned.1.call-done = f32[4096,2048]{1,0:T(8,128)} async-done(((f32[1024,2048]{1,0:T(8,128)}), f32[4096,2048]{1,0:T(8,128)}) %all-gather.20.cloned.1.call-update) | async-done | bytes 33554448 | tf_op jit(solution)/shard_map/all_gather | solution.py:211
  949.3 16.8 reduce_sum.115
  966.1 7.2 multiply_reduce_fusion
  973.4 10.1 fusion.17
  983.5 6.7 fusion.32
  995.7 8.6 fusion.40
  1006.5 12.2 fusion.3
  1018.7 12.0 fusion
  1030.7 30.2 %fusion.2 = (bf16[2,4,512,1024]{2,3,1,0:T(8,128)(2,1)}, bf16[2,4,512,1024]{2,3,1,0:T(8,128)(2,1)}) fusion(f32[2,1024,512,4]{2,1,3,0:T(8,128)} %get-tuple-element.98, f32[2,1024,512,4]{2,1,3,0:T(8,128)} %get-tuple-element.94, f32[2,4,512]{2,1,0:T(4,128)S(1)} %get-tuple-element.97, f32[2,4,512]{2,1,0:T(4,128)S(1)} %bitcast.239, ...), kind=kLoop, calls=%fused_computation.4 | loop fusion | flops 50331648 | bytes 85000192 | tf_op jit(solution)/shard_map/while/body/eval_jaxpr/convert_element_type | solution.py:123
  1060.9 6.8 convolution_bitcast_fusion.2
  1067.8 6.2 fusion.38
  1076.7 7.1 convolution_convert_fusion.4
  1083.9 13.9 convolution_convert_fusion.3
  1116.5 5.9 convolution_convert_fusion.5
  1126.5 124.5 %reduce-scatter.18.cloned.1.call-done = bf16[256,2048]{1,0:T(8,128)(2,1)} async-done(((bf16[2048,2048]{1,0:T(8,128)(2,1)}), bf16[256,2048]{1,0:T(8,128)(2,1)}) %reduce-scatter.18.cloned.1.call-update) | async-done | bytes 1048592 | tf_op jit(solution)/shard_map/reduce_scatter | solution.py:272
  1253.8 147.3 %reduce-scatter.16.cloned.1.call-done = bf16[256,2048]{1,0:T(8,128)(2,1)} async-done(((bf16[2048,2048]{1,0:T(8,128)(2,1)}), bf16[256,2048]{1,0:T(8,128)(2,1)}) %reduce-scatter.16.cloned.1.call-update) | async-done | bytes 1048592 | tf_op jit(solution)/shard_map/reduce_scatter | solution.py:269
  1403.9 62.9 %reduce-scatter.12.cloned.1.call-done = bf16[256,128]{1,0:T(8,128)(2,1)} async-done(((bf16[2048,128]{1,0:T(8,128)(2,1)}), bf16[256,128]{1,0:T(8,128)(2,1)}) %reduce-scatter.12.cloned.1.call-update) | async-done | bytes 65552 | tf_op jit(solution)/shard_map/reduce_scatter | solution.py:260
  1468.3 63.9 %reduce-scatter.10.cloned.1.call-done = bf16[256,128]{1,0:T(8,128)(2,1)} async-done(((bf16[2048,128]{1,0:T(8,128)(2,1)}), bf16[256,128]{1,0:T(8,128)(2,1)}) %reduce-scatter.10.cloned.1.call-update) | async-done | bytes 65552 | tf_op jit(solution)/shard_map/reduce_scatter | solution.py:257
  1533.7 70.0 %reduce-scatter.14.cloned.1.call-done = bf16[512,256]{1,0:T(8,128)(2,1)} async-done(((bf16[512,2048]{1,0:T(8,128)(2,1)}), bf16[512,256]{1,0:T(8,128)(2,1)}) %reduce-scatter.14.cloned.1.call-update) | async-done | bytes 262160 | tf_op jit(solution)/shard_map/reduce_scatter | solution.py:263
  1605.5 152.6 %all-reduce.13.cloned.1.call-done = (bf16[1024,2048]{1,0:T(8,128)(2,1)}, bf16[1024,2048]{1,0:T(8,128)(2,1)}) async-done(((bf16[1024,2048]{1,0:T(8,128)(2,1)}, bf16[1024,2048]{1,0:T(8,128)(2,1)}), (bf16[1024,2048]{1,0:T(8,128)(2,1)}, bf16[1024,2048]{1,0:T(8,128)(2,1)})) %all-reduce.13.cloned.1.call-update) | async-done | bytes 8388624 | tf_op jit(solution)/shard_map/psum | solution.py:200
  1758.1 5.9 fusion.13
  1764.0 21.9 %all-reduce.6 = (bf16[2048]{0:T(1024)(128)(2,1)S(1)}, bf16[2048]{0:T(1024)(128)(2,1)S(1)}) all-reduce(bf16[2048]{0:T(1024)(128)(2,1)S(1)} %get-tuple-element.54, bf16[2048]{0:T(1024)(128)(2,1)S(1)} %get-tuple-element.52), channel_id=3, replica_groups=mesh['dp'=8,'tensor'=4] {'dp'}, use_global_device_ids=true, to_apply=%region_17.18.clone | all-reduce | flops 4096 | bytes 16384
  1787.2 8.5 add_convert_fusion.1
  1795.8 6.8 fusion.18
  1802.6 27.5 %reduce-scatter.8.cloned.1.call-done = bf16[256,512]{1,0:T(8,128)(2,1)} async-done(((bf16[2048,512]{1,0:T(8,128)(2,1)}), bf16[256,512]{1,0:T(8,128)(2,1)}) %reduce-scatter.8.cloned.1.call-update) | async-done | bytes 262160 | tf_op jit(solution)/shard_map/reduce_scatter | solution.py:254
  (227 shorter events, 84.2 us)
Async XLA Ops:
  7.2 104.9 %all-gather.10.cloned.1.call-start = ((), (), s32[]{:S(2)}) async-start(), calls=%async_computation.7 | async-start | bytes 2359296 | tf_op jit(solution)/shard_map/all_gather | solution.py:161
  7.9 158.8 %all-gather.12.cloned.1.call-start = ((), (), s32[]{:S(2)}) async-start(), calls=%async_computation.8 | async-start | bytes 2359296 | tf_op jit(solution)/shard_map/all_gather | solution.py:164
  8.7 315.8 %all-reduce.11.cloned.1.call-start = ((), (), s32[]{:S(2)}) async-start(), calls=%async_computation.9 | async-start | bytes 16777216 | tf_op jit(solution)/shard_map/psum | solution.py:193
  14.6 96.5 %copy-start.45 = (f32[1024]{0:T(1024)}, f32[1024]{0:T(1024)S(1)}, u32[]{:S(2)}) copy-start(f32[1024]{0:T(1024)S(1)} %fusion.50) | copy-start | bytes 12292
  38.0 73.1 %copy-start.40 = (f32[8,1,256]{2,1,0:T(1,128)}, f32[8,1,256]{2,1,0:T(1,128)S(1)}, u32[]{:S(2)}) copy-start(f32[8,1,256]{2,1,0:T(1,128)S(1)} %convert_element_type.247) | copy-start | bytes 24580
  38.6 65.6 %copy-start.28 = (f32[1,1024,32]{1,2,0:T(8,128)}, f32[1,1024,32]{1,2,0:T(8,128)S(1)}, u32[]{:S(2)}) copy-start(f32[1,1024,32]{1,2,0:T(8,128)S(1)} %get-tuple-element.87) | copy-start | bytes 393220
  38.6 65.6 %copy-start.30 = (f32[1,1024,32]{1,2,0:T(8,128)}, f32[1,1024,32]{1,2,0:T(8,128)S(1)}, u32[]{:S(2)}) copy-start(f32[1,1024,32]{1,2,0:T(8,128)S(1)} %get-tuple-element.88) | copy-start | bytes 393220
  38.6 79.1 %copy-start.24 = (f32[1024,64]{0,1:T(8,128)}, f32[1024,64]{0,1:T(8,128)S(1)}, u32[]{:S(2)}) copy-start(f32[1024,64]{0,1:T(8,128)S(1)} %maximum_bitcast_fusion) | copy-start | bytes 786436
  38.7 79.1 %copy-start.22 = (f32[1024,64]{0,1:T(8,128)}, f32[1024,64]{0,1:T(8,128)S(1)}, u32[]{:S(2)}) copy-start(f32[1024,64]{0,1:T(8,128)S(1)} %maximum_bitcast_fusion.1) | copy-start | bytes 786436
  71.8 39.3 %copy-start.15 = (bf16[2048,128]{1,0:T(8,128)(2,1)}, bf16[2048,128]{1,0:T(8,128)(2,1)S(1)}, u32[]{:S(2)}) copy-start(bf16[2048,128]{1,0:T(8,128)(2,1)S(1)} %all_gather.35) | copy-start | bytes 1572868
  109.6 50.6 %copy-start.26 = (bf16[1024,128]{0,1:T(8,128)(2,1)}, bf16[1024,128]{0,1:T(8,128)(2,1)S(1)}, u32[]{:S(2)}) copy-start(bf16[1024,128]{0,1:T(8,128)(2,1)S(1)} %convolution_convert_fusion.10) | copy-start | bytes 786436
  111.9 40.0 %copy-start.8 = (pred[512,1024]{0,1:T(8,128)(4,1)}, pred[512,1024]{0,1:T(8,128)(4,1)S(1)}, u32[]{:S(2)}) copy-start(pred[512,1024]{0,1:T(8,128)(4,1)S(1)} %get-tuple-element.90) | copy-start | bytes 1572868
  111.9 48.3 %copy-start.6 = (pred[512,1024]{0,1:T(8,128)(4,1)}, pred[512,1024]{0,1:T(8,128)(4,1)S(1)}, u32[]{:S(2)}) copy-start(pred[512,1024]{0,1:T(8,128)(4,1)S(1)} %get-tuple-element.89) | copy-start | bytes 1572868
  112.1 23.4 %copy-start.11 = (bf16[1024,2,64,1]{0,2,3,1:T(8,128)(2,1)}, bf16[1024,2,64,1]{0,2,3,1:T(8,128)(2,1)S(1)}, u32[]{:S(2)}) copy-start(bf16[1024,2,64,1]{0,2,3,1:T(8,128)(2,1)S(1)} %fusion.46) | copy-start | bytes 786436
  118.5 17.0 copy-start.17
  135.4 16.5 copy-start.34
  151.9 10.7 copy-start
  174.3 276.9 %all-gather.16.cloned.1.call-start = ((), (), s32[]{:S(2)}) async-start(), calls=%async_computation.11 | async-start | bytes 9437184 | tf_op jit(solution)/shard_map/all_gather | solution.py:167
  174.9 400.9 %all-gather.14.cloned.1.call-start = ((), (), s32[]{:S(2)}) async-start(), calls=%async_computation.10 | async-start | bytes 9437184 | tf_op jit(solution)/shard_map/all_gather | solution.py:166
  175.4 525.4 %all-gather.18.cloned.1.call-start = ((), (), s32[]{:S(2)}) async-start(), calls=%async_computation.12 | async-start | bytes 9437184 | tf_op jit(solution)/shard_map/all_gather | solution.py:168
  176.0 773.2 %all-gather.20.cloned.1.call-start = ((), (), s32[]{:S(2)}) async-start(), calls=%async_computation.20 | async-start | bytes 41943040 | tf_op jit(solution)/shard_map/all_gather | solution.py:211
  192.4 138.4 %copy-start.38 = (f32[8,1,256]{2,1,0:T(1,128)}, f32[8,1,256]{2,1,0:T(1,128)S(1)}, u32[]{:S(2)}) copy-start(f32[8,1,256]{2,1,0:T(1,128)S(1)} %convert_element_type.248) | copy-start | bytes 24580
  722.7 13.2 copy-start.59
  749.4 374.4 %reduce-scatter.20.cloned.1.call-start = ((), (), s32[]{:S(2)}) async-start(), calls=%async_computation.19 | async-start | bytes 9437184 | tf_op jit(solution)/shard_map/reduce_scatter | solution.py:275
  763.7 487.3 %reduce-scatter.18.cloned.1.call-start = ((), (), s32[]{:S(2)}) async-start(), calls=%async_computation.18 | async-start | bytes 9437184 | tf_op jit(solution)/shard_map/reduce_scatter | solution.py:272
  779.3 621.8 %reduce-scatter.16.cloned.1.call-start = ((), (), s32[]{:S(2)}) async-start(), calls=%async_computation.17 | async-start | bytes 9437184 | tf_op jit(solution)/shard_map/reduce_scatter | solution.py:269
  793.5 673.4 %reduce-scatter.12.cloned.1.call-start = ((), (), s32[]{:S(2)}) async-start(), calls=%async_computation.15 | async-start | bytes 589824 | tf_op jit(solution)/shard_map/reduce_scatter | solution.py:260
  949.3 16.8 copy-start.39
  949.3 16.8 copy-start.44
  973.4 10.1 copy-start.52
  973.4 17.0 slice-start
  973.4 17.0 slice-start.1
  973.4 17.0 slice-start.2
  995.7 8.7 copy-start.4
  995.7 10.8 copy-start.27
  995.7 10.8 copy-start.37
  1004.4 14.4 copy-start.32
  1030.7 30.2 %copy-start.20 = (bf16[1,512,8,64]{1,3,2,0:T(8,128)(2,1)S(1)}, bf16[1,512,8,64]{1,3,2,0:T(8,128)(2,1)}, u32[]{:S(2)}) copy-start(bf16[1,512,8,64]{1,3,2,0:T(8,128)(2,1)} %copy-done.19) | copy-start | bytes 1572868
  1067.8 464.5 %reduce-scatter.10.cloned.1.call-start = ((), (), s32[]{:S(2)}) async-start(), calls=%async_computation.14 | async-start | bytes 589824 | tf_op jit(solution)/shard_map/reduce_scatter | solution.py:257
  1067.8 8.8 copy-start.55
  1067.8 8.8 copy-start.57
  1076.4 527.3 %reduce-scatter.14.cloned.1.call-start = ((), (), s32[]{:S(2)}) async-start(), calls=%async_computation.16 | async-start | bytes 2359296 | tf_op jit(solution)/shard_map/reduce_scatter | solution.py:263
  1083.8 14.0 copy-start.12
  1083.8 674.2 %all-reduce.13.cloned.1.call-start = ((), (), s32[]{:S(2)}) async-start(), calls=%async_computation.21 | async-start | bytes 16777216 | tf_op jit(solution)/shard_map/psum | solution.py:200
  1116.3 713.7 %reduce-scatter.8.cloned.1.call-start = ((), (), s32[]{:S(2)}) async-start(), calls=%async_computation.13 | async-start | bytes 2359296 | tf_op jit(solution)/shard_map/reduce_scatter | solution.py:254
  1122.5 635.6 %copy-start.41 = (f32[8,1,256]{2,1,0:T(1,128)S(1)}, f32[8,1,256]{2,1,0:T(1,128)}, u32[]{:S(2)}) copy-start(f32[8,1,256]{2,1,0:T(1,128)} %copy-done.40) | copy-start | bytes 24580
  1122.5 635.6 %copy-start.46 = (f32[1024]{0:T(1024)S(1)}, f32[1024]{0:T(1024)}, u32[]{:S(2)}) copy-start(f32[1024]{0:T(1024)} %copy-done.45) | copy-start | bytes 12292
  1126.5 660.7 %copy-start.48 = (f32[1024]{0:T(1024)S(1)}, f32[1024]{0:T(1024)}, u32[]{:S(2)}) copy-start(f32[1024]{0:T(1024)} %copy-done.47) | copy-start | bytes 12292
  (31 other events, 149.3 us)
Sparse Core Ops, SparseCore 0:
  10.1 57.9 all-gather.9
  70.1 52.7 all-gather.11
  174.4 150.0 all-reduce.10
  326.5 124.6 all-gather.15
  453.1 122.6 all-gather.13
  577.7 123.1 all-gather.17
  749.5 199.6 all-gather.19
  952.9 147.8 reduce-scatter.19
  1104.5 146.5 reduce-scatter.17
  1254.5 146.5 reduce-scatter.15
  1405.1 61.7 reduce-scatter.11
  1470.6 61.5 reduce-scatter.9
  1535.8 67.8 reduce-scatter.13
  1606.1 151.8 all-reduce.12
  1761.4 68.5 reduce-scatter.7
